TPU v7x, 32 devices: a whole 2x2x4 slice. The times are simulated.
32 devices in a mesh: item: 8 (over z, x), bucket: 4 (over y, core).
Axes of the slice: x: 2, y: 2, z: 4, core: 2. Of those that a mesh axis runs over, the one named last changes fastest.
Arguments:
- code_rows: bfloat16 [8192, 64], P('item'), may hold values from -6 to 6
- centroids: bfloat16 [32768, 64], P('bucket'), may hold values from -0.5 to 0.5
Outputs:
- grad_codes: float32 [8192, 64], P('item')
- new_centroids: float32 [32768, 64], P('bucket')
All inputs are finite; a program needn't handle non-finite values.
Results may differ from a plain program's by a relative error of at most 0.0032.
Values sent between devices are 32-bit elements; how exact they have to be, the bound alone decides.
No kernel may reach another device: no remote copies, remote signals or barrier semaphores. Data moves between devices by JAX's collectives and lax.ppermute only.
A program may use at most 128 MiB of HBM per device.

v0:
```python
import jax
import jax.numpy as jnp
from jax import lax
from jax.sharding import PartitionSpec as P

BUCKETS = 32768
ITERS = 3
score_scale = 20.0
step_rate = 0.2
epsilon = 1e-06


def joined(value, axis, join):
    pieces = jax.tree.map(lambda part: lax.all_gather(part, axis), value)
    head = jax.tree.map(lambda part: part[0], pieces)
    tail = jax.tree.map(lambda part: part[1:], pieces)
    so_far, _ = lax.scan(lambda so_far, piece: (join(so_far, piece), None), head, tail)
    return so_far


def scores_of(code_rows, centroids):
    return score_scale * lax.dot_general(
        code_rows, centroids, (((1,), (1,)), ((), ())), preferred_element_type=jnp.float32
    )


def lse_pair(first, second):
    highest = jnp.maximum(first[0], second[0])
    return (
        highest,
        first[1] * jnp.exp(first[0] - highest) + second[1] * jnp.exp(second[0] - highest),
    )


def stats_triple(first, second):
    highest = jnp.maximum(first[0], second[0])
    return (
        highest,
        first[1] * jnp.exp(first[0] - highest) + second[1] * jnp.exp(second[0] - highest),
        first[2] + second[2],
    )


def reduce_rows(values):
    highest = jnp.max(values, axis=1)
    summed = jnp.sum(jnp.exp(values - highest[:, None]), axis=1)
    highest, summed = joined((highest, summed), "bucket", lse_pair)
    return highest + jnp.log(summed)


def reduce_cols(values):
    highest = jnp.max(values, axis=0)
    summed = jnp.sum(jnp.exp(values - highest[None, :]), axis=0)
    highest, summed = joined((highest, summed), "item", lse_pair)
    return highest + jnp.log(summed)


def rescale(own_rows, gradient):
    moved = own_rows.astype(jnp.float32) - step_rate * gradient
    return moved * lax.rsqrt(jnp.mean(moved * moved, axis=1, keepdims=True) + epsilon)


def body(code_rows, centroids):
    rows_total = code_rows.shape[0] * lax.axis_size("item")
    log_rows = jnp.log(jnp.float32(rows_total))
    log_buckets = jnp.log(jnp.float32(BUCKETS))
    potential_col = jnp.zeros((centroids.shape[0],), jnp.float32)
    potential_row = jnp.zeros((code_rows.shape[0],), jnp.float32)
    for iteration in range(ITERS):
        potential_row = -log_rows - reduce_rows(
            scores_of(code_rows, centroids) + potential_col[None, :]
        )
        potential_col = -log_buckets - reduce_cols(
            scores_of(code_rows, centroids) + potential_row[:, None]
        )
    scores = scores_of(code_rows, centroids)
    plan = jnp.exp(scores + potential_row[:, None] + potential_col[None, :] + log_rows)
    masses = jnp.sum(plan, axis=1)
    highest = jnp.max(scores, axis=1)
    totals = jnp.sum(jnp.exp(scores - highest[:, None]), axis=1)
    highest, totals, masses = joined((highest, totals, masses), "bucket", stats_triple)
    delta = (masses[:, None] * jnp.exp(scores - highest[:, None]) / totals[:, None] - plan).astype(
        jnp.bfloat16
    )
    grad_codes = lax.psum(
        score_scale * jnp.dot(delta, centroids, preferred_element_type=jnp.float32), "bucket"
    )
    local_grad = score_scale * lax.dot_general(
        delta, code_rows, (((0,), (0,)), ((), ())), preferred_element_type=jnp.float32
    )
    gradient = lax.psum(local_grad, "item")
    new_centroids = rescale(centroids, gradient)
    return (grad_codes, new_centroids)


def solution(mesh):
    return jax.shard_map(
        body,
        mesh=mesh,
        in_specs=(P("item", None), P("bucket", None)),
        out_specs=(P("item", None), P("bucket", None)),
        check_vma=False,
    )
```

profile of v0, /device:TPU:0, one launch (start us, length us, event | category | flops | bytes accessed | tf_op | source)
XLA Modules:
  0.0 586.0 jit_solution(3918211216739394180)
XLA Ops:
  8.1 14.3 %fusion.2 = (f32[1024]{0:T(1024)S(1)}, f32[1024,8192]{1,0:T(8,128)}) fusion(bf16[1024,64]{0,1:T(8,128)(2,1)S(1)} %copy-done, bf16[8192,64]{0,1:T(8,128)(2,1)} %param.17), kind=kOutput, calls=%fused_computation.49 | convolution fusion | flops 1090518016 | bytes 34738176 | tf_op jit(solution)/shard_map/dot_general | solution.py:22
  22.4 6.2 %all-gather = f32[4096]{0:T(1024)S(1)} all-gather(f32[1024]{0:T(1024)S(1)} %get-tuple-element.326), channel_id=2, replica_groups=mesh['item'=8,'bucket'=4] {'bucket'}, dimensions={0}, use_global_device_ids=true | all-gather | bytes 20480 | tf_op jit(solution)/shard_map/all_gather | solution.py:14
  28.6 13.6 %exponential_reduce_fusion.5 = f32[1024]{0:T(1024)S(1)} fusion(f32[1024,8192]{1,0:T(8,128)} %get-tuple-element.327, f32[1024]{0:T(1024)S(1)} %get-tuple-element.326), kind=kLoop, calls=%fused_computation.29 | loop fusion | flops 16776192 | bytes 33562624 | tf_op jit(solution)/shard_map/reduce_sum | solution.py:80
  42.3 5.4 all-gather.1
  47.9 12.5 %add_reduce_fusion.3 = f32[8192]{0:T(1024)S(1)} fusion(f32[1024,8192]{1,0:T(8,128)} %get-tuple-element.327, f32[1024]{0:T(1024)S(1)} %add_subtract_fusion.5), kind=kLoop, calls=%fused_computation.33 | loop fusion | flops 16769024 | bytes 33591296 | tf_op jit(solution)/shard_map/reduce_max | solution.py:52
  60.4 14.0 %exponential_reduce_fusion.4 = f32[8192]{0:T(1024)S(1)} fusion(f32[1024,8192]{1,0:T(8,128)} %get-tuple-element.327, f32[8192]{0:T(1024)S(1)} %add_reduce_fusion.3, f32[1024]{0:T(1024)S(1)} %add_subtract_fusion.5), kind=kLoop, calls=%fused_computation.28 | loop fusion | flops 25157632 | bytes 33624064 | tf_op jit(solution)/shard_map/reduce_sum | solution.py:53
  74.4 31.4 %all-gather.2 = f32[65536]{0:T(1024)S(1)} all-gather(f32[8192]{0:T(1024)S(1)} %add_reduce_fusion.3), channel_id=4, replica_groups=mesh['item'=8,'bucket'=4] {'item'}, dimensions={0}, use_global_device_ids=true | all-gather | bytes 294912 | tf_op jit(solution)/shard_map/all_gather | solution.py:14
  105.8 30.7 %all-gather.3 = f32[65536]{0:T(1024)S(1)} all-gather(f32[8192]{0:T(1024)S(1)} %exponential_reduce_fusion.4), channel_id=5, replica_groups=mesh['item'=8,'bucket'=4] {'item'}, dimensions={0}, use_global_device_ids=true | all-gather | bytes 294912 | tf_op jit(solution)/shard_map/all_gather | solution.py:14
  137.6 12.2 %add_reduce_fusion.2 = f32[1024]{0:T(1024)S(1)} fusion(f32[1024,8192]{1,0:T(8,128)} %get-tuple-element.327, f32[8192]{0:T(1024)S(1)} %add_subtract_fusion.2), kind=kLoop, calls=%fused_computation.32 | loop fusion | flops 16776192 | bytes 33591296 | tf_op jit(solution)/shard_map/reduce_max | solution.py:45
  149.8 14.3 %exponential_reduce_fusion.3 = f32[1024]{0:T(1024)S(1)} fusion(f32[1024,8192]{1,0:T(8,128)} %get-tuple-element.327, f32[1024]{0:T(1024)S(1)} %add_reduce_fusion.2, f32[8192]{0:T(1024)S(1)} %add_subtract_fusion.2), kind=kLoop, calls=%fused_computation.27 | loop fusion | flops 25164800 | bytes 33595392 | tf_op jit(solution)/shard_map/reduce_sum | solution.py:46
  164.1 5.2 all-gather.4
  169.3 5.2 all-gather.5
  174.7 12.5 %add_reduce_fusion.1 = f32[8192]{0:T(1024)S(1)} fusion(f32[1024,8192]{1,0:T(8,128)} %get-tuple-element.327, f32[1024]{0:T(1024)S(1)} %add_subtract_fusion.4), kind=kLoop, calls=%fused_computation.31 | loop fusion | flops 16769024 | bytes 33591296 | tf_op jit(solution)/shard_map/reduce_max | solution.py:52
  187.2 14.0 %exponential_reduce_fusion.2 = f32[8192]{0:T(1024)S(1)} fusion(f32[1024,8192]{1,0:T(8,128)} %get-tuple-element.327, f32[8192]{0:T(1024)S(1)} %add_reduce_fusion.1, f32[1024]{0:T(1024)S(1)} %add_subtract_fusion.4), kind=kLoop, calls=%fused_computation.26 | loop fusion | flops 25157632 | bytes 33624064 | tf_op jit(solution)/shard_map/reduce_sum | solution.py:53
  201.2 30.9 %all-gather.6 = f32[65536]{0:T(1024)S(1)} all-gather(f32[8192]{0:T(1024)S(1)} %add_reduce_fusion.1), channel_id=8, replica_groups=mesh['item'=8,'bucket'=4] {'item'}, dimensions={0}, use_global_device_ids=true | all-gather | bytes 294912 | tf_op jit(solution)/shard_map/all_gather | solution.py:14
  232.1 30.7 %all-gather.7 = f32[65536]{0:T(1024)S(1)} all-gather(f32[8192]{0:T(1024)S(1)} %exponential_reduce_fusion.2), channel_id=9, replica_groups=mesh['item'=8,'bucket'=4] {'item'}, dimensions={0}, use_global_device_ids=true | all-gather | bytes 294912 | tf_op jit(solution)/shard_map/all_gather | solution.py:14
  263.9 12.2 %add_reduce_fusion = f32[1024]{0:T(1024)S(1)} fusion(f32[1024,8192]{1,0:T(8,128)} %get-tuple-element.327, f32[8192]{0:T(1024)S(1)} %add_subtract_fusion.1), kind=kLoop, calls=%fused_computation.30 | loop fusion | flops 16776192 | bytes 33591296 | tf_op jit(solution)/shard_map/reduce_max | solution.py:45
  276.1 14.3 %exponential_reduce_fusion.1 = f32[1024]{0:T(1024)S(1)} fusion(f32[1024,8192]{1,0:T(8,128)} %get-tuple-element.327, f32[1024]{0:T(1024)S(1)} %add_reduce_fusion, f32[8192]{0:T(1024)S(1)} %add_subtract_fusion.1), kind=kLoop, calls=%fused_computation.25 | loop fusion | flops 25164800 | bytes 33595392 | tf_op jit(solution)/shard_map/reduce_sum | solution.py:46
  290.4 5.2 all-gather.8
  295.6 5.4 all-gather.9
  301.2 12.5 %add_reduce_fusion.4 = f32[8192]{0:T(1024)S(1)} fusion(f32[1024,8192]{1,0:T(8,128)} %get-tuple-element.327, f32[1024]{0:T(1024)S(1)} %add_subtract_fusion.3), kind=kLoop, calls=%fused_computation.34 | loop fusion | flops 16769024 | bytes 33591296 | tf_op jit(solution)/shard_map/reduce_max | solution.py:52
  313.7 14.0 %exponential_reduce_fusion = f32[8192]{0:T(1024)S(1)} fusion(f32[1024,8192]{1,0:T(8,128)} %get-tuple-element.327, f32[8192]{0:T(1024)S(1)} %add_reduce_fusion.4, f32[1024]{0:T(1024)S(1)} %add_subtract_fusion.3), kind=kLoop, calls=%fused_computation.24 | loop fusion | flops 25157632 | bytes 33624064 | tf_op jit(solution)/shard_map/reduce_sum | solution.py:53
  327.7 30.9 %all-gather.10 = f32[65536]{0:T(1024)S(1)} all-gather(f32[8192]{0:T(1024)S(1)} %add_reduce_fusion.4), channel_id=12, replica_groups=mesh['item'=8,'bucket'=4] {'item'}, dimensions={0}, use_global_device_ids=true | all-gather | bytes 294912 | tf_op jit(solution)/shard_map/all_gather | solution.py:14
  358.6 30.7 %all-gather.11 = f32[65536]{0:T(1024)S(1)} all-gather(f32[8192]{0:T(1024)S(1)} %exponential_reduce_fusion), channel_id=13, replica_groups=mesh['item'=8,'bucket'=4] {'item'}, dimensions={0}, use_global_device_ids=true | all-gather | bytes 294912 | tf_op jit(solution)/shard_map/all_gather | solution.py:14
  390.4 14.8 %fusion = f32[1024]{0:T(1024)S(1)} fusion(f32[1024,8192]{1,0:T(8,128)} %get-tuple-element.327, f32[8192]{0:T(1024)S(1)} %add_subtract_fusion, f32[1024]{0:T(1024)S(1)} %add_subtract_fusion.3), kind=kLoop, calls=%fused_computation.35 | loop fusion | flops 33553408 | bytes 33595392 | tf_op jit(solution)/shard_map/reduce_sum | solution.py:78
  405.2 5.2 all-gather.12
  410.7 18.8 %subtract_convert_fusion = bf16[1024,8192]{1,0:T(8,128)(2,1)S(1)} fusion(f32[1024,8192]{1,0:T(8,128)} %get-tuple-element.327, f32[1024]{0:T(1024)S(1)} %get-tuple-element.223, f32[1024]{0:T(1024)S(1)} %get-tuple-element.222, f32[1024]{0:T(1024)S(1)} %get-tuple-element.221, f32[8192]{0:T(1024)S(1)} %add_subtract_fusion, f32[1024]{0:T(1024)S(1)} %add_subtract_fusion.3), kind=kLoop, calls=%fused_computation.22 | loop fusion | flops 67108864 | bytes 50380800 | tf_op jit(solution)/shard_map/convert_element_type | solution.py:82
  429.5 5.7 copy-done.1
  435.2 4.3 convolution_multiply_fusion
  439.8 11.7 %convolution_multiply_fusion.1 = f32[1024,64]{0,1:T(8,128)} fusion(bf16[1024,8192]{1,0:T(8,128)(2,1)} %copy-done.1, bf16[8192,64]{0,1:T(8,128)(2,1)S(1)} %copy-done.2), kind=kOutput, calls=%fused_computation.41 | convolution fusion | flops 1073807360 | bytes 18087936 | tf_op jit(solution)/shard_map/dot_general | solution.py:86
  451.5 91.4 %all-reduce.5.cloned.1.call-done = f32[8192,64]{0,1:T(8,128)} async-done(((f32[8192,64]{0,1:T(8,128)}), f32[8192,64]{0,1:T(8,128)}) %all-reduce.5.cloned.1.call-update) | async-done | bytes 2097168 | tf_op jit(solution)/shard_map/psum | solution.py:91
  548.2 29.2 %all-reduce.3.cloned.1.call-done = f32[1024,64]{0,1:T(8,128)} async-done(((f32[1024,64]{0,1:T(8,128)}), f32[1024,64]{0,1:T(8,128)}) %all-reduce.3.cloned.1.call-update) | async-done | bytes 262160 | tf_op jit(solution)/shard_map/psum | solution.py:85
  (139 shorter events, 14.7 us)
Async XLA Ops:
  7.2 0.9 copy-start
  7.2 535.8 %all-reduce.5.cloned.1.call-start = ((), (), s32[]{:S(2)}) async-start(), calls=%async_computation.1 | async-start | bytes 4194304 | tf_op jit(solution)/shard_map/psum | solution.py:91
  410.6 29.2 %copy-start.2 = (bf16[8192,64]{0,1:T(8,128)(2,1)S(1)}, bf16[8192,64]{0,1:T(8,128)(2,1)}, u32[]{:S(2)}) copy-start(bf16[8192,64]{0,1:T(8,128)(2,1)} %param.17) | copy-start | bytes 3145732
  429.5 5.7 copy-start.1
  439.5 137.9 %all-reduce.3.cloned.1.call-start = ((), (), s32[]{:S(2)}) async-start(), calls=%async_computation | async-start | bytes 524288 | tf_op jit(solution)/shard_map/psum | solution.py:85
Sparse Core Ops, SparseCore 0:
  439.7 103.2 all-reduce.4
  545.9 31.5 all-reduce.2
where the time goes:
time: 588 us; the launch traced here: 586 us
  blocking collectives  223 us (38%)
  other arithmetic  186 us (32%)
  waiting for transfers between devices  121 us (21%)
  matrix products  30.3 us (5%)
  between operations  14.4 us (2%)
  local copies, waits for them, and re-layouts  10.4 us (2%)
    all_gather x13, blocking collectives, joined(): pieces = jax.tree.map(lambda part: lax.all_gather(part, axis), value)  223 us
    psum x1, waiting for transfers between devices, body(): gradient = lax.psum(local_grad, 'item')  91.4 us
    reduce_sum x3, other arithmetic, reduce_cols(): summed = jnp.sum(jnp.exp(values - highest[None, :]), axis=0)  41.9 us
    reduce_max x3, other arithmetic, reduce_cols(): highest = jnp.max(values, axis=0)  37.4 us
    psum x1, waiting for transfers between devices, body(): lax.psum(score_scale * jnp.dot(delta, centroids, preferred_element_type=j...  29.2 us
    reduce_sum x2, other arithmetic, reduce_rows(): summed = jnp.sum(jnp.exp(values - highest[:, None]), axis=1)  28.6 us
    reduce_max x2, other arithmetic, reduce_rows(): highest = jnp.max(values, axis=1)  24.3 us
    convert_element_type x1, other arithmetic, body(): (masses[:, None] * jnp.exp(scores - highest[:, None]) / totals[:, None] -...  18.8 us
  transfers between devices with their start and end apart: 2, of which 2 were waited for; matrix products, arithmetic and copies ran while one was open for 3% of the time, Pallas kernels for 0%

commit v1 on v0

--- a/solution.py
+++ b/solution.py
@@ -82,8 +82,11 @@
     delta = (masses[:, None] * jnp.exp(scores - highest[:, None]) / totals[:, None] - plan).astype(
         jnp.bfloat16
     )
-    grad_codes = lax.psum(
-        score_scale * jnp.dot(delta, centroids, preferred_element_type=jnp.float32), "bucket"
+    grad_codes = jnp.sum(
+        lax.all_gather(
+            score_scale * jnp.dot(delta, centroids, preferred_element_type=jnp.float32), "bucket"
+        ),
+        axis=0,
     )
     local_grad = score_scale * lax.dot_general(
         delta, code_rows, (((0,), (0,)), ((), ())), preferred_element_type=jnp.float32

time: 588 us -> 569 us (0.968)
  waiting for transfers between devices: 121 us -> 99.7 us
    psum x1 -> x0, waiting for transfers between devices: 29.2 us -> none  [body(): lax.psum(score_scale * jnp.dot(delta, centroids, preferred_element_type=j...]
    all_gather x0 -> x1, waiting for transfers between devices: none -> 7.38 us  [body(): lax.all_gather(score_scale * jnp.dot(delta, centroids, preferred_element_...]
  transfers between devices with their start and end apart: 2 -> 2, of which waited for: 2 -> 2; matrix products, arithmetic and copies ran while one was open for 3% -> 2% of each run, Pallas kernels for 0% -> 0%
where the time goes in v1:
time: 569 us; the launch traced here: 568 us
  blocking collectives  223 us (39%)
  other arithmetic  187 us (33%)
  waiting for transfers between devices  99.7 us (18%)
  matrix products  30.3 us (5%)
  between operations  15.8 us (3%)
  local copies, waits for them, and re-layouts  10.6 us (2%)
    all_gather x13, blocking collectives, joined(): pieces = jax.tree.map(lambda part: lax.all_gather(part, axis), value)  223 us
    psum x1, waiting for transfers between devices, body(): gradient = lax.psum(local_grad, 'item')  92.3 us
    reduce_sum x3, other arithmetic, reduce_cols(): summed = jnp.sum(jnp.exp(values - highest[None, :]), axis=0)  41.9 us
    reduce_max x3, other arithmetic, reduce_cols(): highest = jnp.max(values, axis=0)  37.4 us
    reduce_sum x2, other arithmetic, reduce_rows(): summed = jnp.sum(jnp.exp(values - highest[:, None]), axis=1)  28.6 us
    reduce_max x2, other arithmetic, reduce_rows(): highest = jnp.max(values, axis=1)  24.4 us
    convert_element_type x1, other arithmetic, body(): (masses[:, None] * jnp.exp(scores - highest[:, None]) / totals[:, None] -...  18.7 us
    reduce_sum x1, other arithmetic, body(): masses = jnp.sum(plan, axis=1)  14.6 us
  transfers between devices with their start and end apart: 2, of which 2 were waited for; matrix products, arithmetic and copies ran while one was open for 2% of the time, Pallas kernels for 0%

profile of v1, /device:TPU:0, one launch (start us, length us, event | category | flops | bytes accessed | tf_op | source)
XLA Modules:
  0.0 567.8 jit_solution(10975580398263308968)
XLA Ops:
  8.9 14.3 %fusion.2 = (f32[1024]{0:T(1024)S(1)}, f32[1024,8192]{1,0:T(8,128)}) fusion(bf16[1024,64]{0,1:T(8,128)(2,1)S(1)} %copy-done, bf16[8192,64]{0,1:T(8,128)(2,1)} %param.17), kind=kOutput, calls=%fused_computation.49 | convolution fusion | flops 1090518016 | bytes 34738176 | tf_op jit(solution)/shard_map/dot_general | solution.py:22
  23.2 6.3 %all-gather = f32[4096]{0:T(1024)S(1)} all-gather(f32[1024]{0:T(1024)S(1)} %get-tuple-element.326), channel_id=2, replica_groups=mesh['item'=8,'bucket'=4] {'bucket'}, dimensions={0}, use_global_device_ids=true | all-gather | bytes 20480 | tf_op jit(solution)/shard_map/all_gather | solution.py:14
  29.5 13.6 %exponential_reduce_fusion.5 = f32[1024]{0:T(1024)S(1)} fusion(f32[1024,8192]{1,0:T(8,128)} %get-tuple-element.327, f32[1024]{0:T(1024)S(1)} %get-tuple-element.326), kind=kLoop, calls=%fused_computation.29 | loop fusion | flops 16776192 | bytes 33562624 | tf_op jit(solution)/shard_map/reduce_sum | solution.py:80
  43.1 5.4 all-gather.1
  48.8 12.5 %add_reduce_fusion.3 = f32[8192]{0:T(1024)S(1)} fusion(f32[1024,8192]{1,0:T(8,128)} %get-tuple-element.327, f32[1024]{0:T(1024)S(1)} %add_subtract_fusion.5), kind=kLoop, calls=%fused_computation.33 | loop fusion | flops 16769024 | bytes 33591296 | tf_op jit(solution)/shard_map/reduce_max | solution.py:52
  61.2 14.0 %exponential_reduce_fusion.4 = f32[8192]{0:T(1024)S(1)} fusion(f32[1024,8192]{1,0:T(8,128)} %get-tuple-element.327, f32[8192]{0:T(1024)S(1)} %add_reduce_fusion.3, f32[1024]{0:T(1024)S(1)} %add_subtract_fusion.5), kind=kLoop, calls=%fused_computation.28 | loop fusion | flops 25157632 | bytes 33624064 | tf_op jit(solution)/shard_map/reduce_sum | solution.py:53
  75.2 31.4 %all-gather.2 = f32[65536]{0:T(1024)S(1)} all-gather(f32[8192]{0:T(1024)S(1)} %add_reduce_fusion.3), channel_id=4, replica_groups=mesh['item'=8,'bucket'=4] {'item'}, dimensions={0}, use_global_device_ids=true | all-gather | bytes 294912 | tf_op jit(solution)/shard_map/all_gather | solution.py:14
  106.6 30.7 %all-gather.3 = f32[65536]{0:T(1024)S(1)} all-gather(f32[8192]{0:T(1024)S(1)} %exponential_reduce_fusion.4), channel_id=5, replica_groups=mesh['item'=8,'bucket'=4] {'item'}, dimensions={0}, use_global_device_ids=true | all-gather | bytes 294912 | tf_op jit(solution)/shard_map/all_gather | solution.py:14
  138.5 12.2 %add_reduce_fusion.2 = f32[1024]{0:T(1024)S(1)} fusion(f32[1024,8192]{1,0:T(8,128)} %get-tuple-element.327, f32[8192]{0:T(1024)S(1)} %add_subtract_fusion.2), kind=kLoop, calls=%fused_computation.32 | loop fusion | flops 16776192 | bytes 33591296 | tf_op jit(solution)/shard_map/reduce_max | solution.py:45
  150.7 14.3 %exponential_reduce_fusion.3 = f32[1024]{0:T(1024)S(1)} fusion(f32[1024,8192]{1,0:T(8,128)} %get-tuple-element.327, f32[1024]{0:T(1024)S(1)} %add_reduce_fusion.2, f32[8192]{0:T(1024)S(1)} %add_subtract_fusion.2), kind=kLoop, calls=%fused_computation.27 | loop fusion | flops 25164800 | bytes 33595392 | tf_op jit(solution)/shard_map/reduce_sum | solution.py:46
  165.0 5.2 all-gather.4
  170.2 5.2 all-gather.5
  175.6 12.5 %add_reduce_fusion.1 = f32[8192]{0:T(1024)S(1)} fusion(f32[1024,8192]{1,0:T(8,128)} %get-tuple-element.327, f32[1024]{0:T(1024)S(1)} %add_subtract_fusion.4), kind=kLoop, calls=%fused_computation.31 | loop fusion | flops 16769024 | bytes 33591296 | tf_op jit(solution)/shard_map/reduce_max | solution.py:52
  188.0 14.0 %exponential_reduce_fusion.2 = f32[8192]{0:T(1024)S(1)} fusion(f32[1024,8192]{1,0:T(8,128)} %get-tuple-element.327, f32[8192]{0:T(1024)S(1)} %add_reduce_fusion.1, f32[1024]{0:T(1024)S(1)} %add_subtract_fusion.4), kind=kLoop, calls=%fused_computation.26 | loop fusion | flops 25157632 | bytes 33624064 | tf_op jit(solution)/shard_map/reduce_sum | solution.py:53
  202.0 30.9 %all-gather.6 = f32[65536]{0:T(1024)S(1)} all-gather(f32[8192]{0:T(1024)S(1)} %add_reduce_fusion.1), channel_id=8, replica_groups=mesh['item'=8,'bucket'=4] {'item'}, dimensions={0}, use_global_device_ids=true | all-gather | bytes 294912 | tf_op jit(solution)/shard_map/all_gather | solution.py:14
  232.9 30.7 %all-gather.7 = f32[65536]{0:T(1024)S(1)} all-gather(f32[8192]{0:T(1024)S(1)} %exponential_reduce_fusion.2), channel_id=9, replica_groups=mesh['item'=8,'bucket'=4] {'item'}, dimensions={0}, use_global_device_ids=true | all-gather | bytes 294912 | tf_op jit(solution)/shard_map/all_gather | solution.py:14
  264.7 12.2 %add_reduce_fusion = f32[1024]{0:T(1024)S(1)} fusion(f32[1024,8192]{1,0:T(8,128)} %get-tuple-element.327, f32[8192]{0:T(1024)S(1)} %add_subtract_fusion.1), kind=kLoop, calls=%fused_computation.30 | loop fusion | flops 16776192 | bytes 33591296 | tf_op jit(solution)/shard_map/reduce_max | solution.py:45
  276.9 14.3 %exponential_reduce_fusion.1 = f32[1024]{0:T(1024)S(1)} fusion(f32[1024,8192]{1,0:T(8,128)} %get-tuple-element.327, f32[1024]{0:T(1024)S(1)} %add_reduce_fusion, f32[8192]{0:T(1024)S(1)} %add_subtract_fusion.1), kind=kLoop, calls=%fused_computation.25 | loop fusion | flops 25164800 | bytes 33595392 | tf_op jit(solution)/shard_map/reduce_sum | solution.py:46
  291.2 5.2 all-gather.8
  296.5 5.4 all-gather.9
  302.0 12.5 %add_reduce_fusion.4 = f32[8192]{0:T(1024)S(1)} fusion(f32[1024,8192]{1,0:T(8,128)} %get-tuple-element.327, f32[1024]{0:T(1024)S(1)} %add_subtract_fusion.3), kind=kLoop, calls=%fused_computation.34 | loop fusion | flops 16769024 | bytes 33591296 | tf_op jit(solution)/shard_map/reduce_max | solution.py:52
  314.5 14.0 %exponential_reduce_fusion = f32[8192]{0:T(1024)S(1)} fusion(f32[1024,8192]{1,0:T(8,128)} %get-tuple-element.327, f32[8192]{0:T(1024)S(1)} %add_reduce_fusion.4, f32[1024]{0:T(1024)S(1)} %add_subtract_fusion.3), kind=kLoop, calls=%fused_computation.24 | loop fusion | flops 25157632 | bytes 33624064 | tf_op jit(solution)/shard_map/reduce_sum | solution.py:53
  328.5 30.9 %all-gather.10 = f32[65536]{0:T(1024)S(1)} all-gather(f32[8192]{0:T(1024)S(1)} %add_reduce_fusion.4), channel_id=12, replica_groups=mesh['item'=8,'bucket'=4] {'item'}, dimensions={0}, use_global_device_ids=true | all-gather | bytes 294912 | tf_op jit(solution)/shard_map/all_gather | solution.py:14
  359.4 30.7 %all-gather.11 = f32[65536]{0:T(1024)S(1)} all-gather(f32[8192]{0:T(1024)S(1)} %exponential_reduce_fusion), channel_id=13, replica_groups=mesh['item'=8,'bucket'=4] {'item'}, dimensions={0}, use_global_device_ids=true | all-gather | bytes 294912 | tf_op jit(solution)/shard_map/all_gather | solution.py:14
  391.2 14.6 %fusion = f32[1024]{0:T(1024)S(1)} fusion(f32[1024,8192]{1,0:T(8,128)} %get-tuple-element.327, f32[8192]{0:T(1024)S(1)} %add_subtract_fusion, f32[1024]{0:T(1024)S(1)} %add_subtract_fusion.3), kind=kLoop, calls=%fused_computation.35 | loop fusion | flops 33553408 | bytes 33595392 | tf_op jit(solution)/shard_map/reduce_sum | solution.py:78
  405.8 5.3 all-gather.12
  411.4 18.7 %subtract_convert_fusion = bf16[1024,8192]{1,0:T(8,128)(2,1)S(1)} fusion(f32[1024,8192]{1,0:T(8,128)} %get-tuple-element.327, f32[1024]{0:T(1024)S(1)} %get-tuple-element.223, f32[1024]{0:T(1024)S(1)} %get-tuple-element.222, f32[1024]{0:T(1024)S(1)} %get-tuple-element.221, f32[8192]{0:T(1024)S(1)} %add_subtract_fusion, f32[1024]{0:T(1024)S(1)} %add_subtract_fusion.3), kind=kLoop, calls=%fused_computation.22 | loop fusion | flops 67108864 | bytes 50380800 | tf_op jit(solution)/shard_map/convert_element_type | solution.py:82
  430.1 5.7 %copy-done.1 = bf16[1024,8192]{1,0:T(8,128)(2,1)} copy-done((bf16[1024,8192]{1,0:T(8,128)(2,1)}, bf16[1024,8192]{1,0:T(8,128)(2,1)S(1)}, u32[]{:S(2)}) %copy-start.1) | copy-done | bytes 16777240
  435.8 5.9 %convolution_multiply_fusion.1 = f32[1024,64]{0,1:T(8,128)} fusion(bf16[1024,8192]{1,0:T(8,128)(2,1)S(1)} %subtract_convert_fusion, bf16[8192,64]{0,1:T(8,128)(2,1)S(1)} %copy-done.2), kind=kOutput, calls=%fused_computation.41 | convolution fusion | flops 1073807360 | bytes 18087936 | tf_op jit(solution)/shard_map/dot_general | solution.py:87
  442.1 10.1 %convolution_multiply_fusion = f32[8192,64]{0,1:T(8,128)} fusion(bf16[1024,64]{0,1:T(8,128)(2,1)S(1)} %copy-done, bf16[1024,8192]{1,0:T(8,128)(2,1)} %copy-done.1), kind=kOutput, calls=%fused_computation.37 | convolution fusion | flops 1074266112 | bytes 19005440 | tf_op jit(solution)/shard_map/dot_general | solution.py:91
  452.2 7.4 %all-gather.16.cloned.1.call-done = f32[4096,64]{0,1:T(8,128)} async-done(((f32[1024,64]{0,1:T(8,128)}), f32[4096,64]{0,1:T(8,128)}) %all-gather.16.cloned.1.call-update) | async-done | bytes 1048592 | tf_op jit(solution)/shard_map/all_gather | solution.py:86
  462.9 92.3 %all-reduce.2.cloned.1.call-done = f32[8192,64]{0,1:T(8,128)} async-done(((f32[8192,64]{0,1:T(8,128)}), f32[8192,64]{0,1:T(8,128)}) %all-reduce.2.cloned.1.call-update) | async-done | bytes 2097168 | tf_op jit(solution)/shard_map/psum | solution.py:94
  (140 shorter events, 16.3 us)
Async XLA Ops:
  8.0 0.9 copy-start
  8.0 451.6 %all-gather.16.cloned.1.call-start = ((), (), s32[]{:S(2)}) async-start(), calls=%async_computation.1 | async-start | bytes 1310720 | tf_op jit(solution)/shard_map/all_gather | solution.py:86
  405.8 30.0 %copy-start.2 = (bf16[8192,64]{0,1:T(8,128)(2,1)S(1)}, bf16[8192,64]{0,1:T(8,128)(2,1)}, u32[]{:S(2)}) copy-start(bf16[8192,64]{0,1:T(8,128)(2,1)} %param.17) | copy-start | bytes 3145732
  430.1 5.7 %copy-start.1 = (bf16[1024,8192]{1,0:T(8,128)(2,1)}, bf16[1024,8192]{1,0:T(8,128)(2,1)S(1)}, u32[]{:S(2)}) copy-start(bf16[1024,8192]{1,0:T(8,128)(2,1)S(1)} %subtract_convert_fusion) | copy-start | bytes 50331652
  441.8 113.4 %all-reduce.2.cloned.1.call-start = ((), (), s32[]{:S(2)}) async-start(), calls=%async_computation | async-start | bytes 4194304 | tf_op jit(solution)/shard_map/psum | solution.py:94
Sparse Core Ops, SparseCore 0:
  441.9 17.6 all-gather.15
Sparse Core Ops, SparseCore 1:
  452.3 102.8 all-reduce.1
